TPU v7x, 32 devices: a whole 2x2x4 slice. The times are simulated.
32 devices in a mesh: group: 4 (over y, x), hash: 8 (over z, core).
Axes of the slice: x: 2, y: 2, z: 4, core: 2. Of those that a mesh axis runs over, the one named last changes fastest.
Arguments:
- pooled: bfloat16 [8, 512, 32, 256], P('hash', 'group'), may hold values from -0.375 to 0.375
- weight: bfloat16 [1024, 2048], replicated, may hold values from -0.1875 to 0.1875
- cotangent: bfloat16 [8, 512, 2048], P('hash', 'group'), may hold values from -6 to 6
- owners: int32 [8, 32, 512, 2], P('hash', 'group'), may hold values from 0 to 7, all different within a row; in each aligned block of 4096 rows (0 to 4095, 4096 to 8191, ..., all dimensions but the last counted through in order) at most 1365 rows name the same one
- local_rows: int32 [8, 32, 512, 2], P('hash', 'group'), may hold values from 0 to 511
- table: float32 [32, 4096, 256], P('group', 'hash'), may hold values from -0.625 to 0.625
- accum: float32 [32, 4096], P('group', 'hash'), may hold values from 0.05 to 2
Outputs:
- wgrad: bfloat16 [1024, 2048], replicated
- table_out: float32 [32, 4096, 256], P('group', 'hash')
- accum_out: float32 [32, 4096], P('group', 'hash')
Inputs may be any that keep to these rules, and one draw needn't show every extreme that they name: Among the rows of one device (aligned blocks of 4096 bags), no owner is named more than 1365 times, a bound that some block reaches; the 2 owners of one bag differ.
All inputs are finite; a program needn't handle non-finite values.
Results may differ from a plain program's by a relative error of at most 0.0059.
Values may be sent and summed in bfloat16 or wider, within the bound.
No kernel may reach another device: no remote copies, remote signals or barrier semaphores. Data moves between devices by JAX's collectives and lax.ppermute only.
A program may use at most 128 MiB of HBM per device.

v0:
```python
import math
import jax
import jax.numpy as jnp
from jax import lax
from jax.sharding import PartitionSpec as P


def local(pooled, weight, cotangent, owners, local_rows, table, accum):
    vectors = pooled[0]
    samples, feats, width = vectors.shape
    inter = jnp.einsum("sfe,sge->sfg", vectors, vectors, preferred_element_type=jnp.float32).astype(
        jnp.bfloat16
    )
    inter_rows = inter.reshape(samples, feats * feats)
    preact = jnp.dot(inter_rows, weight, preferred_element_type=jnp.float32)
    sigmoid_v = jax.nn.sigmoid(preact)
    dpre = (
        cotangent[0].astype(jnp.float32) * (sigmoid_v * (1.0 + preact * (1.0 - sigmoid_v)))
    ).astype(jnp.bfloat16)
    dinter = lax.dot_general(
        dpre, weight, (((1,), (1,)), ((), ())), preferred_element_type=jnp.float32
    ).reshape(samples, feats, feats)
    dsym = (dinter + jnp.swapaxes(dinter, 1, 2)).astype(jnp.bfloat16)
    dpooled = jnp.einsum("sfg,sge->fse", dsym, vectors, preferred_element_type=jnp.float32).astype(
        jnp.bfloat16
    )
    exchanged = lax.all_to_all(dpooled, "group", split_axis=0, concat_axis=1, tiled=True)
    wlocal = lax.dot_general(
        inter_rows, dpre, (((0,), (0,)), ((), ())), preferred_element_type=jnp.float32
    )
    total_samples = samples * lax.axis_size("group") * lax.axis_size("hash")
    wgrad = (lax.psum(wlocal, ("group", "hash")) / math.sqrt(total_samples)).astype(jnp.bfloat16)
    owner_ids = owners[0]
    row_ids = local_rows[0]
    groups_local, rows_dev = accum.shape
    hashes = lax.axis_size("hash")
    feature_index = jnp.arange(groups_local, dtype=jnp.int32)[:, None, None]
    values = jnp.broadcast_to(exchanged[:, :, None, :], owner_ids.shape + (width,)).reshape(
        -1, width
    )
    dense_keys = (feature_index * (hashes * rows_dev) + owner_ids * rows_dev + row_ids).reshape(-1)
    partial_grad = jax.ops.segment_sum(
        values.astype(jnp.float32), dense_keys, num_segments=groups_local * hashes * rows_dev
    )
    rowgrad = lax.psum_scatter(
        partial_grad.reshape(groups_local, hashes * rows_dev, width).astype(jnp.bfloat16),
        "hash",
        scatter_dimension=1,
        tiled=True,
    ).astype(jnp.float32)
    accum_out = accum + jnp.mean(rowgrad * rowgrad, axis=-1)
    table_out = table - 0.1 * rowgrad / jnp.sqrt(accum_out)[:, :, None]
    return (wgrad, table_out, accum_out)


def solution(mesh):
    in_specs = (
        P("hash", "group", None, None),
        P(),
        P("hash", "group", None),
        P("hash", "group", None, None),
        P("hash", "group", None, None),
        P("group", "hash", None),
        P("group", "hash"),
    )
    out_specs = (P(), P("group", "hash", None), P("group", "hash"))
    return jax.shard_map(local, mesh=mesh, in_specs=in_specs, out_specs=out_specs, check_vma=False)
```

profile of v0, /device:TPU:0, one launch (start us, length us, event | category | flops | bytes accessed | tf_op | source)
XLA Modules:
  0.0 382.3 jit_solution(6259762305518760065)
XLA Ops:
  8.0 0.0 copy-start
  8.0 0.0 all-reduce.2.cloned.1.call-start
  8.1 1.5 copy-done
  9.6 0.7 fusion.11
  10.3 1.1 copy.25
  11.4 0.0 copy-start.2
  11.4 3.0 fusion.27
  14.4 0.0 copy-done.2
  14.4 4.6 %fusion.17 = f32[1024,2048]{1,0:T(8,128)} fusion(bf16[128,1024]{0,1:T(8,128)(2,1)S(1)} %bitcast.47, f32[128,2048]{1,0:T(8,128)S(1)} %fusion.27, bf16[1,128,2048]{2,1,0:T(8,128)(2,1)S(1)} %copy-done.2), kind=kOutput, calls=%fused_computation.19 | convolution fusion | flops 539492352 | bytes 10223616 | tf_op jit(solution)/shard_map/dot_general | solution.py:28
  18.9 0.0 all-reduce.2.cloned.1.call-update
  19.0 3.7 fusion.15
  22.7 0.3 fusion.21
  23.0 1.4 copy.30
  24.5 0.7 convert_bitcast_fusion.1
  25.1 0.0 copy-start.4
  25.2 2.6 copy.31
  27.7 5.1 %all-to-all-start = ((bf16[32,128,256]{2,1,0:T(8,128)(2,1)}), bf16[32,128,256]{2,1,0:T(8,128)(2,1)S(1)}, u32[]{:S(2)}, u32[]{:S(2)}) async-start(bf16[32,128,256]{2,1,0:T(8,128)(2,1)} %copy.31), calls=%async_computation | async-start | bytes 4194304 | tf_op jit(solution)/shard_map/all_to_all | solution.py:27
  32.9 0.0 reduce-scatter.2.cloned.1.call-start
  32.9 0.0 copy-done.4
  32.9 0.0 copy-start.3
  32.9 2.0 copy.26
  34.9 3.1 mul.48
  38.0 1.5 add.47
  39.6 3.0 add.48
  42.6 0.0 copy-done.3
  42.6 2.0 copy.27
  44.6 3.0 squeeze.9
  47.7 20.9 %all-to-all-done = bf16[32,128,256]{2,1,0:T(8,128)(2,1)S(1)} async-done(((bf16[32,128,256]{2,1,0:T(8,128)(2,1)}), bf16[32,128,256]{2,1,0:T(8,128)(2,1)S(1)}, u32[]{:S(2)}, u32[]{:S(2)}) %all-to-all-start) | async-done | bytes 2097184 | tf_op jit(solution)/shard_map/all_to_all | solution.py:27
  68.6 0.5 convert_bitcast_fusion
  69.1 0.4 copy.32
  69.6 4.5 %broadcast_in_dim.5 = f32[8,512,2,256]{3,2,1,0:T(2,128)} broadcast(f32[8,512,256]{2,1,0:T(8,128)S(1)} %bitcast.44), dimensions={0,1,3} | broadcast | bytes 12582912 | tf_op jit(solution)/shard_map/broadcast_in_dim | solution.py:38
  74.0 11.1 %reshape.73 = f32[8192,256]{1,0:T(8,128)} reshape(f32[8,512,2,256]{3,2,1,0:T(2,128)} %broadcast_in_dim.5) | data formatting | bytes 16777216 | tf_op jit(solution)/shard_map/convert_element_type | solution.py:43
  85.2 58.1 %scatter_custom_fusion = f32[32768,256]{1,0:T(8,128)} fusion(s32[8192]{0:T(1024)S(1)} %bitcast.49, f32[8192,256]{1,0:T(8,128)} %reshape.73, f32[]{:T(128)} %constant.3.clone.1), kind=kCustom, calls=%fused_computation.1 | custom fusion | flops 2097152 | bytes 33554944 | tf_op jit(solution)/shard_map/scatter-add | solution.py:42
  143.3 17.5 %convert_element_type.62 = bf16[32768,256]{1,0:T(8,128)(2,1)} convert(f32[32768,256]{1,0:T(8,128)} %scatter_custom_fusion) | non-fusion elementwise | flops 8388608 | bytes 50331648 | tf_op jit(solution)/shard_map/convert_element_type | solution.py:46
  160.7 0.0 reduce-scatter.2.cloned.1.call-update
  160.8 0.0 copy-start.5
  160.8 115.0 %all-reduce.2.cloned.1.call-done = f32[1024,2048]{1,0:T(8,128)} async-done(((f32[1024,2048]{1,0:T(8,128)}), f32[1024,2048]{1,0:T(8,128)}) %all-reduce.2.cloned.1.call-update) | async-done | bytes 8388624 | tf_op jit(solution)/shard_map/psum | solution.py:32
  275.7 6.6 %multiply_convert_fusion = bf16[1024,2048]{1,0:T(8,128)(2,1)} fusion(f32[1024,2048]{1,0:T(8,128)} %all-reduce.2.cloned.1.call-done), kind=kLoop, calls=%fused_computation.3 | loop fusion | flops 4194304 | bytes 12582912 | tf_op jit(solution)/shard_map/convert_element_type | solution.py:32
  282.3 85.0 %reduce-scatter.2.cloned.1.call-done = bf16[8,512,256]{2,1,0:T(8,128)(2,1)} async-done(((bf16[8,4096,256]{2,1,0:T(8,128)(2,1)}), bf16[8,512,256]{2,1,0:T(8,128)(2,1)}) %reduce-scatter.2.cloned.1.call-update) | async-done | bytes 2097168 | tf_op jit(solution)/shard_map/reduce_scatter | solution.py:45
  367.4 2.2 fusion.4
  369.6 0.0 copy-done.5
  369.6 0.6 fusion.26
  370.2 0.0 copy-start.1
  370.2 4.6 %fusion.3 = f32[8,512,256]{2,1,0:T(8,128)} fusion(f32[8,512,256]{2,1,0:T(8,128)} %param.12, bf16[8,512,256]{2,1,0:T(8,128)(2,1)} %reduce-scatter.2.cloned.1.call-done, f32[8,512]{1,0:T(8,128)S(1)} %get-tuple-element.3), kind=kLoop, calls=%fused_computation.7 | loop fusion | flops 4194304 | bytes 10502144 | tf_op jit(solution)/shard_map/sub | solution.py:52
  374.8 0.0 copy-done.1
  (3 shorter events, 0.1 us)
Async XLA Ops:
  8.0 1.6 copy-start
  8.0 267.7 %all-reduce.2.cloned.1.call-start = ((), (), s32[]{:S(2)}) async-start(), calls=%async_computation.2 | async-start | bytes 16777216 | tf_op jit(solution)/shard_map/psum | solution.py:32
  11.4 3.0 copy-start.2
  25.1 7.7 %copy-start.4 = (s32[1,8,512,2]{2,3,1,0:T(2,128)S(1)}, s32[1,8,512,2]{2,3,1,0:T(2,128)}, u32[]{:S(2)}) copy-start(s32[1,8,512,2]{2,3,1,0:T(2,128)} %param.10) | copy-start | bytes 98308
  27.7 40.9 %all-to-all-start = ((bf16[32,128,256]{2,1,0:T(8,128)(2,1)}), bf16[32,128,256]{2,1,0:T(8,128)(2,1)S(1)}, u32[]{:S(2)}, u32[]{:S(2)}) async-start(bf16[32,128,256]{2,1,0:T(8,128)(2,1)} %copy.31), calls=%async_computation | async-start | bytes 4194304 | tf_op jit(solution)/shard_map/all_to_all | solution.py:27
  32.9 334.5 %reduce-scatter.2.cloned.1.call-start = ((), (), s32[]{:S(2)}) async-start(), calls=%async_computation.3 | async-start | bytes 18874368 | tf_op jit(solution)/shard_map/reduce_scatter | solution.py:45
  32.9 9.7 %copy-start.3 = (s32[1,8,512,2]{2,3,1,0:T(2,128)S(1)}, s32[1,8,512,2]{2,3,1,0:T(2,128)}, u32[]{:S(2)}) copy-start(s32[1,8,512,2]{2,3,1,0:T(2,128)} %param.11) | copy-start | bytes 98308
  160.8 208.8 %copy-start.5 = (f32[8,512]{1,0:T(8,128)S(1)}, f32[8,512]{1,0:T(8,128)}, u32[]{:S(2)}) copy-start(f32[8,512]{1,0:T(8,128)} %param.13) | copy-start | bytes 49156
  370.2 4.6 %copy-start.1 = (bf16[1,128,32,256]{3,2,1,0:T(8,128)(2,1)S(1)}, bf16[1,128,32,256]{3,2,1,0:T(8,128)(2,1)}, u32[]{:S(2)}) copy-start(bf16[1,128,32,256]{3,2,1,0:T(8,128)(2,1)} %param.7) | copy-start | bytes 6291460
Sparse Core Ops, SparseCore 0:
  19.1 256.6 all-reduce.1
Sparse Core Ops, SparseCore 1:
  160.8 206.5 reduce-scatter.1
where the time goes:
time: 383 us; the launch traced here: 382 us
  waiting for transfers between devices  221 us (58%)
  other arithmetic  90.5 us (24%)
  local copies, waits for them, and re-layouts  37.4 us (10%)
  between operations  15.6 us (4%)
  matrix products  12.6 us (3%)
  starting transfers between devices  5.15 us (1%)
    psum x1, waiting for transfers between devices, local(): lax.psum(wlocal, ('group', 'hash')) / math.sqrt(total_samples)  115 us
    reduce_scatter x1, waiting for transfers between devices, local(): lax.psum_scatter(partial_grad.reshape(groups_local, hashes * rows_dev, wi...  85 us
    scatter-add x1, other arithmetic, local(): jax.ops.segment_sum(values.astype(jnp.float32), dense_keys, num_segments=...  58.1 us
    all_to_all x1, waiting for transfers between devices, local(): lax.all_to_all(dpooled, 'group', split_axis=0, concat_axis=1, tiled=True)  20.9 us
    convert_element_type x1, other arithmetic, local(): partial_grad.reshape(groups_local, hashes * rows_dev, width)  17.5 us
    convert_element_type x2, local copies, waits for them, and re-layouts, local(): values.astype(jnp.float32)  11.6 us
  transfers between devices with their start and end apart: 3, of which 3 were waited for; matrix products, arithmetic and copies ran while one was open for 32% of the time, Pallas kernels for 0%

commit v1 on v0

--- a/solution.py
+++ b/solution.py
@@ -29,7 +29,9 @@
         inter_rows, dpre, (((0,), (0,)), ((), ())), preferred_element_type=jnp.float32
     )
     total_samples = samples * lax.axis_size("group") * lax.axis_size("hash")
-    wgrad = (lax.psum(wlocal, ("group", "hash")) / math.sqrt(total_samples)).astype(jnp.bfloat16)
+    wgrad = (lax.psum(lax.psum(wlocal, "hash"), "group") / math.sqrt(total_samples)).astype(
+        jnp.bfloat16
+    )
     owner_ids = owners[0]
     row_ids = local_rows[0]
     groups_local, rows_dev = accum.shape

time: 383 us -> 581 us (1.52)
  waiting for transfers between devices: 221 us -> 420 us
    psum x1 -> x2, waiting for transfers between devices: 115 us -> 222 us  [the longest x1 178 us: local(): lax.psum(wlocal, 'hash')]
    reduce_scatter x1, waiting for transfers between devices: 85 us -> 165 us  [local(): lax.psum_scatter(partial_grad.reshape(groups_local, hashes * rows_dev, wi...]
    all_to_all x1, waiting for transfers between devices: 20.9 us -> 33.3 us  [local(): lax.all_to_all(dpooled, 'group', split_axis=0, concat_axis=1, tiled=True)]
  transfers between devices with their start and end apart: 3 -> 4, of which waited for: 3 -> 4; matrix products, arithmetic and copies ran while one was open for 32% -> 21% of each run, Pallas kernels for 0% -> 0%
where the time goes in v1:
time: 581 us; the launch traced here: 580 us
  waiting for transfers between devices  420 us (72%)
  other arithmetic  92 us (16%)
  local copies, waits for them, and re-layouts  37.1 us (6%)
  between operations  13.9 us (2%)
  matrix products  12.6 us (2%)
    psum x1, waiting for transfers between devices, local(): lax.psum(wlocal, 'hash')  178 us
    reduce_scatter x1, waiting for transfers between devices, local(): lax.psum_scatter(partial_grad.reshape(groups_local, hashes * rows_dev, wi...  165 us
    scatter-add x1, other arithmetic, local(): jax.ops.segment_sum(values.astype(jnp.float32), dense_keys, num_segments=...  58.9 us
    psum x1, waiting for transfers between devices, local(): lax.psum(lax.psum(wlocal, 'hash'), 'group') / math.sqrt(total_samples)  44 us
    all_to_all x1, waiting for transfers between devices, local(): lax.all_to_all(dpooled, 'group', split_axis=0, concat_axis=1, tiled=True)  33.3 us
    convert_element_type x1, other arithmetic, local(): partial_grad.reshape(groups_local, hashes * rows_dev, width)  18.2 us
  transfers between devices with their start and end apart: 4, of which 4 were waited for; matrix products, arithmetic and copies ran while one was open for 21% of the time, Pallas kernels for 0%

profile of v1, /device:TPU:0, one launch (start us, length us, event | category | flops | bytes accessed | tf_op | source)
XLA Modules:
  0.0 580.0 jit_solution(16090727430445273600)
XLA Ops:
  7.2 0.0 copy-start
  7.2 0.0 all-reduce.3.cloned.1.call-start
  7.2 1.5 copy-done
  8.8 0.7 fusion.11
  9.4 1.1 copy.25
  10.5 0.0 copy-start.2
  10.5 3.0 fusion.27
  13.5 0.0 copy-done.2
  13.5 4.6 fusion.17
  18.1 0.0 all-reduce.3.cloned.1.call-update
  18.1 0.0 all-reduce.5.cloned.1.call-start
  18.2 178.4 %all-reduce.3.cloned.1.call-done = f32[1024,2048]{1,0:T(8,128)} async-done(((f32[1024,2048]{1,0:T(8,128)}), f32[1024,2048]{1,0:T(8,128)}) %all-reduce.3.cloned.1.call-update) | async-done | bytes 8388624 | tf_op jit(solution)/shard_map/psum | solution.py:32
  196.5 0.0 all-reduce.5.cloned.1.call-update
  196.6 3.7 fusion.15
  200.3 0.3 fusion.21
  200.6 1.4 copy.30
  202.1 0.7 convert_bitcast_fusion.1
  202.7 0.0 copy-start.4
  202.8 2.5 copy.31
  205.3 3.6 all-to-all-start
  208.9 0.2 reduce-scatter.2.cloned.1.call-start
  209.1 0.0 copy-done.4
  209.1 0.0 copy-start.3
  209.2 2.0 copy.26
  211.1 3.0 mul.48
  214.2 1.5 add.49
  215.7 3.0 add.50
  218.8 0.0 copy-done.3
  218.8 2.0 copy.27
  220.7 3.0 squeeze.9
  223.9 33.3 %all-to-all-done = bf16[32,128,256]{2,1,0:T(8,128)(2,1)S(1)} async-done(((bf16[32,128,256]{2,1,0:T(8,128)(2,1)}), bf16[32,128,256]{2,1,0:T(8,128)(2,1)S(1)}, u32[]{:S(2)}, u32[]{:S(2)}) %all-to-all-start) | async-done | bytes 2097184 | tf_op jit(solution)/shard_map/all_to_all | solution.py:27
  257.2 0.5 convert_bitcast_fusion
  257.7 0.4 copy.32
  258.1 4.5 broadcast_in_dim.5
  262.6 10.9 %reshape.73 = f32[8192,256]{1,0:T(8,128)} reshape(f32[8,512,2,256]{3,2,1,0:T(2,128)} %broadcast_in_dim.5) | data formatting | bytes 16777216 | tf_op jit(solution)/shard_map/convert_element_type | solution.py:45
  273.5 58.9 %scatter_custom_fusion = f32[32768,256]{1,0:T(8,128)} fusion(s32[8192]{0:T(1024)S(1)} %bitcast.49, f32[8192,256]{1,0:T(8,128)} %reshape.73, f32[]{:T(128)} %constant.3.clone.1), kind=kCustom, calls=%fused_computation.1 | custom fusion | flops 2097152 | bytes 33554944 | tf_op jit(solution)/shard_map/scatter-add | solution.py:44
  332.4 18.2 %convert_element_type.62 = bf16[32768,256]{1,0:T(8,128)(2,1)} convert(f32[32768,256]{1,0:T(8,128)} %scatter_custom_fusion) | non-fusion elementwise | flops 8388608 | bytes 50331648 | tf_op jit(solution)/shard_map/convert_element_type | solution.py:48
  350.7 0.0 reduce-scatter.2.cloned.1.call-update
  350.7 0.0 copy-start.5
  350.7 44.0 %all-reduce.5.cloned.1.call-done = f32[1024,2048]{1,0:T(8,128)} async-done(((f32[1024,2048]{1,0:T(8,128)}), f32[1024,2048]{1,0:T(8,128)}) %all-reduce.5.cloned.1.call-update) | async-done | bytes 8388624 | tf_op jit(solution)/shard_map/psum | solution.py:32
  394.7 6.5 %multiply_convert_fusion = bf16[1024,2048]{1,0:T(8,128)(2,1)} fusion(f32[1024,2048]{1,0:T(8,128)} %all-reduce.5.cloned.1.call-done), kind=kLoop, calls=%fused_computation.3 | loop fusion | flops 4194304 | bytes 12582912 | tf_op jit(solution)/shard_map/convert_element_type | solution.py:32
  401.3 164.7 %reduce-scatter.2.cloned.1.call-done = bf16[8,512,256]{2,1,0:T(8,128)(2,1)} async-done(((bf16[8,4096,256]{2,1,0:T(8,128)(2,1)}), bf16[8,512,256]{2,1,0:T(8,128)(2,1)}) %reduce-scatter.2.cloned.1.call-update) | async-done | bytes 2097168 | tf_op jit(solution)/shard_map/reduce_scatter | solution.py:47
  566.0 2.2 fusion.4
  568.2 0.0 copy-done.5
  568.2 0.6 fusion.26
  568.8 0.0 copy-start.1
  568.8 4.6 fusion.3
  573.5 0.0 copy-done.1
  (3 shorter events, 0.1 us)
Async XLA Ops:
  7.2 1.6 copy-start
  7.2 189.4 %all-reduce.3.cloned.1.call-start = ((), (), s32[]{:S(2)}) async-start(), calls=%async_computation.2 | async-start | bytes 16777216 | tf_op jit(solution)/shard_map/psum | solution.py:32
  10.5 3.0 copy-start.2
  18.1 376.6 %all-reduce.5.cloned.1.call-start = ((), (), s32[]{:S(2)}) async-start(), calls=%async_computation.3 | async-start | bytes 16777216 | tf_op jit(solution)/shard_map/psum | solution.py:32
  202.7 6.4 %copy-start.4 = (s32[1,8,512,2]{2,3,1,0:T(2,128)S(1)}, s32[1,8,512,2]{2,3,1,0:T(2,128)}, u32[]{:S(2)}) copy-start(s32[1,8,512,2]{2,3,1,0:T(2,128)} %param.10) | copy-start | bytes 98308
  205.3 51.9 %all-to-all-start = ((bf16[32,128,256]{2,1,0:T(8,128)(2,1)}), bf16[32,128,256]{2,1,0:T(8,128)(2,1)S(1)}, u32[]{:S(2)}, u32[]{:S(2)}) async-start(bf16[32,128,256]{2,1,0:T(8,128)(2,1)} %copy.31), calls=%async_computation | async-start | bytes 4194304 | tf_op jit(solution)/shard_map/all_to_all | solution.py:27
  208.9 357.1 %reduce-scatter.2.cloned.1.call-start = ((), (), s32[]{:S(2)}) async-start(), calls=%async_computation.4 | async-start | bytes 18874368 | tf_op jit(solution)/shard_map/reduce_scatter | solution.py:47
  209.1 9.6 %copy-start.3 = (s32[1,8,512,2]{2,3,1,0:T(2,128)S(1)}, s32[1,8,512,2]{2,3,1,0:T(2,128)}, u32[]{:S(2)}) copy-start(s32[1,8,512,2]{2,3,1,0:T(2,128)} %param.11) | copy-start | bytes 98308
  350.7 217.5 %copy-start.5 = (f32[8,512]{1,0:T(8,128)S(1)}, f32[8,512]{1,0:T(8,128)}, u32[]{:S(2)}) copy-start(f32[8,512]{1,0:T(8,128)} %param.13) | copy-start | bytes 49156
  568.8 4.6 copy-start.1
Sparse Core Ops, SparseCore 0:
  18.3 178.2 all-reduce.2
  200.1 194.6 all-reduce.4
  397.1 168.8 reduce-scatter.1
